TPU v7x, 32 devices: a whole 2x2x4 slice. The times are simulated.
32 devices in a mesh: ev: 16 (over z, y, core), st: 2 (over x).
Axes of the slice: x: 2, y: 2, z: 4, core: 2. Of those that a mesh axis runs over, the one named last changes fastest.
Arguments:
- strain: bfloat16 [2, 6, 256, 4096], P(None, None, 'ev'), may hold values from -0.068359375 to 0.068359375
- green: bfloat16 [2, 3, 256, 6, 4096], P(None, None, 'st', None, 'ev'), may hold values from -6 to 6
- weights: bfloat16 [2, 3, 256, 256], P(None, None, 'ev', 'st'), may hold values from -0.15625 to 0.15625
- mask: int32 [256, 256], P('ev', 'st'), may hold values 0 or 1
Outputs:
- kernels: float32 [2, 4096], P(None, ('ev', 'st'))
All inputs are finite; a program needn't handle non-finite values. No bound on the sum of `mask` on one device may be relied on, other than what follows from the above.
Results may differ from a plain program's by a relative error of at most 0.0003.
Values may be sent and summed in bfloat16 or wider, within the bound.
No kernel may reach another device: no remote copies, remote signals or barrier semaphores. Data moves between devices by JAX's collectives and lax.ppermute only.
A program may use at most 128 MiB of HBM per device.

v0:
```python
import jax
import jax.numpy as jnp
from jax import lax
from jax.sharding import PartitionSpec as P


def local(strain, green, weights, mask):
    masked = weights * mask.astype(jnp.bfloat16)[None, None]
    cells_dev = green.shape[4]
    station_count = green.shape[2]
    event_rows = strain.shape[2]
    ev_count = lax.axis_size("ev")
    st_count = lax.axis_size("st")
    sub_cells = cells_dev // st_count
    shaped = strain.reshape(2, 6, event_rows, ev_count, st_count, sub_cells)
    selected = lax.dynamic_index_in_dim(shaped, lax.axis_index("st"), 4, keepdims=False)
    selected = selected.reshape(2, 6, event_rows, ev_count * sub_cells)
    narrow = lax.all_to_all(selected, "ev", split_axis=3, concat_axis=2, tiled=True)
    strain_all = lax.all_gather(narrow, "st", axis=3, tiled=True)
    green_flat = green.reshape(2, 3, station_count, 6 * cells_dev)
    voigt = jnp.array([1.0, 1.0, 1.0, 2.0, 2.0, 2.0], jnp.float32)
    weight_rows = lax.all_gather(masked, "ev", axis=2, tiled=True)
    row_count = weight_rows.shape[2]
    products = jnp.einsum(
        "rfps,qfsn->rqpn", weight_rows, green_flat, preferred_element_type=jnp.float32
    )
    held_real = (products[0, 0] - products[1, 1]).reshape(row_count, 6, cells_dev)
    held_imag = (products[0, 1] + products[1, 0]).reshape(row_count, 6, cells_dev)
    strain_rows = strain_all.astype(jnp.float32)
    strain_real = jnp.swapaxes(strain_rows[0], 0, 1)
    strain_imag = jnp.swapaxes(strain_rows[1], 0, 1)
    trace_term = jnp.sum(
        strain_real[:, :3].sum(1) * held_real[:, :3].sum(1)
        - strain_imag[:, :3].sum(1) * held_imag[:, :3].sum(1),
        axis=0,
    )
    shear_term = jnp.sum(
        (strain_real * held_real - strain_imag * held_imag) * voigt[None, :, None], axis=(0, 1)
    )
    partial_value = jnp.stack([trace_term, shear_term])
    return lax.psum_scatter(partial_value, "st", scatter_dimension=1, tiled=True)


def solution(mesh):
    placed = (
        P(None, None, "ev", None),
        P(None, None, "st", None, "ev"),
        P(None, None, "ev", "st"),
        P("ev", "st"),
    )
    return jax.shard_map(
        local, mesh=mesh, in_specs=placed, out_specs=P(None, ("ev", "st")), check_vma=False
    )
```

profile of v0, /device:TPU:0, one launch (start us, length us, event | category | flops | bytes accessed | tf_op | source)
XLA Modules:
  0.0 143.1 jit_solution(11234989107015068082)
XLA Ops:
  6.5 2.8 %reshape.20 = bf16[2,6,16,16,2,128]{5,4,3,2,1,0:T(2,128)(2,1)S(1)} reshape(bf16[2,6,16,4096]{3,2,1,0:T(8,128)(2,1)} %param.5) | data formatting | bytes 3145728 | tf_op jit(solution)/shard_map/reshape | solution.py:15
  9.4 1.9 %constant_dynamic-slice_fusion = bf16[2,6,16,16,1,128]{5,4,3,2,1,0:T(2,128)(2,1)S(1)} fusion(bf16[2,6,16,16,2,128]{5,4,3,2,1,0:T(2,128)(2,1)S(1)} %reshape.20, s32[]{:T(128)S(6)} %select_n.4), kind=kLoop, calls=%fused_computation.14 | loop fusion | bytes 1572868 | tf_op jit(solution)/shard_map/jit(dynamic_index_in_dim)/dynamic_slice | solution.py:16
  11.3 11.5 %copy.44 = bf16[2,6,16,16,1,128]{2,0,1,5,3,4:T(2,128)(2,1)} copy(bf16[2,6,16,16,1,128]{5,4,3,2,1,0:T(2,128)(2,1)S(1)} %constant_dynamic-slice_fusion) | data formatting | bytes 1572864 | tf_op jit(solution)/shard_map/reshape | solution.py:17
  22.8 18.4 %reshape.28 = bf16[16,2,12288]{2,1,0:T(2,128)(2,1)} reshape(bf16[2048,6,2,16]{3,2,1,0:T(2,128)(2,1)} %bitcast.43) | data formatting | bytes 1572864
  41.2 7.5 %all-to-all-start = ((bf16[16,2,12288]{2,1,0:T(2,128)(2,1)}), bf16[16,2,12288]{2,1,0:T(2,128)(2,1)S(1)}, u32[]{:S(2)}, u32[]{:S(2)}) async-start(bf16[16,2,12288]{2,1,0:T(2,128)(2,1)} %reshape.28), calls=%async_computation | async-start | bytes 1572864 | tf_op jit(solution)/shard_map/all_to_all | solution.py:18
  48.7 0.0 all-gather.2.cloned.1.call-start
  48.8 3.1 %copy.33 = bf16[2,3,128,6,256]{2,4,3,1,0:T(8,128)(2,1)S(1)} copy(bf16[2,3,128,6,256]{4,2,3,1,0:T(8,128)(2,1)} %param.6) | data formatting | bytes 4718592 | tf_op args[1]
  51.9 15.5 %all-to-all-done = bf16[16,2,12288]{2,1,0:T(2,128)(2,1)S(1)} async-done(((bf16[16,2,12288]{2,1,0:T(2,128)(2,1)}), bf16[16,2,12288]{2,1,0:T(2,128)(2,1)S(1)}, u32[]{:S(2)}, u32[]{:S(2)}) %all-to-all-start) | async-done | bytes 786464 | tf_op jit(solution)/shard_map/all_to_all | solution.py:18
  67.4 5.6 %reshape.29 = bf16[2048,6,2,16]{3,2,1,0:T(2,128)(2,1)} reshape(bf16[16,2,12288]{2,1,0:T(2,128)(2,1)S(1)} %all-to-all-done) | data formatting | bytes 1572864
  73.0 14.8 %copy.46 = bf16[2,6,16,16,128]{4,2,3,1,0:T(8,128)(2,1)} copy(bf16[2,6,16,16,128]{2,0,1,4,3:T(2,128)(2,1)} %bitcast.42) | data formatting | bytes 1572864 | tf_op jit(solution)/shard_map/all_to_all | solution.py:18
  87.9 0.0 reduce-scatter.4.cloned.1.call-start
  88.0 22.4 %all_gather.7 = bf16[2,3,256,128]{3,2,1,0:T(8,128)(2,1)S(1)} all-gather(bf16[2,3,16,128]{3,2,1,0:T(8,128)(2,1)S(1)} %broadcast_multiply_fusion), channel_id=1, replica_groups=mesh['ev'=16,'st'=2] {'ev'}, dimensions={2}, use_global_device_ids=true | all-gather | bytes 417792 | tf_op jit(solution)/shard_map/all_gather | solution.py:22
  110.4 1.8 %convolution_bitcast_fusion = f32[2,2,256,1536]{3,2,1,0:T(8,128)S(1)} fusion(bf16[2,3,128,1536,1]{2,3,1,0,4:T(8,128)(2,1)S(1)} %bitcast.48, bf16[2,3,256,128]{3,2,1,0:T(8,128)(2,1)S(1)} %all_gather.7), kind=kOutput, calls=%fused_computation | convolution fusion | flops 1207959552 | bytes 9043968 | tf_op jit(solution)/shard_map/rfps,qfsn->rqpn/dot_general | solution.py:24
  112.2 1.7 %slice_subtract_fusion = (f32[1,1,256,1536]{3,2,1,0:T(8,128)}, f32[1,1,256,1536]{3,2,1,0:T(8,128)S(1)}) fusion(f32[2,2,256,1536]{3,2,1,0:T(8,128)S(1)} %convolution_bitcast_fusion), kind=kLoop, calls=%fused_computation.3 | loop fusion | flops 786432 | bytes 9437184 | tf_op jit(solution)/shard_map/sub | solution.py:27
  113.9 1.9 %copy.35 = f32[1,1,256,1536]{2,3,1,0:T(8,128)S(1)} copy(f32[1,1,256,1536]{3,2,1,0:T(8,128)} %get-tuple-element.5) | data formatting | bytes 3145728 | tf_op jit(solution)/shard_map/sub | solution.py:27
  115.8 1.6 %copy.39 = f32[256,6,256]{2,0,1:T(8,128)} copy(f32[256,6,256]{0,2,1:T(8,128)S(1)} %bitcast.44) | data formatting | bytes 3145728 | tf_op jit(solution)/shard_map/sub | solution.py:27
  117.4 0.8 slice_reduce_fusion.2
  118.2 1.1 copy.36
  119.3 0.5 copy.37
  119.8 0.5 copy.40
  120.2 0.8 slice_reduce_fusion
  121.0 1.1 copy.38
  122.1 0.0 all-gather.2.cloned.1.call-done
  122.1 1.7 %convert_element_type.6 = f32[2,6,256,256]{3,2,1,0:T(8,128)S(1)} convert(bf16[2,6,256,256]{3,2,1,0:T(8,128)(2,1)} %all-gather.2.cloned.1.call-done) | non-fusion elementwise | flops 786432 | bytes 4718592 | tf_op jit(solution)/shard_map/convert_element_type | solution.py:29
  123.8 0.2 slice_bitcast_fusion.1
  124.1 0.1 slice_reduce_fusion.1
  124.2 1.3 copy-done
  125.5 0.7 multiply_reduce_fusion
  126.1 0.1 subtract_reduce_fusion
  126.2 0.8 copy.48
  127.0 7.8 %reduce-scatter.4.cloned.1.call-done = f32[128,2]{1,0:T(8,128)} async-done(((f32[256,2]{1,0:T(8,128)}), f32[128,2]{1,0:T(8,128)}) %reduce-scatter.4.cloned.1.call-update) | async-done | bytes 1040
  134.8 1.5 %copy.49 = f32[2,128]{1,0:T(2,128)} copy(f32[2,128]{0,1:T(8,128)} %bitcast.51) | data formatting | bytes 2048
  (12 shorter events, 0.1 us)
Async XLA Ops:
  41.2 7.6 %copy-start.2 = (s32[16,128]{1,0:T(8,128)S(1)}, s32[16,128]{1,0:T(8,128)}, u32[]{:S(2)}) copy-start(s32[16,128]{1,0:T(8,128)} %param.8) | copy-start | bytes 24580
  41.2 26.2 %all-to-all-start = ((bf16[16,2,12288]{2,1,0:T(2,128)(2,1)}), bf16[16,2,12288]{2,1,0:T(2,128)(2,1)S(1)}, u32[]{:S(2)}, u32[]{:S(2)}) async-start(bf16[16,2,12288]{2,1,0:T(2,128)(2,1)} %reshape.28), calls=%async_computation | async-start | bytes 1572864 | tf_op jit(solution)/shard_map/all_to_all | solution.py:18
  48.7 73.4 %all-gather.2.cloned.1.call-start = ((), (), s32[]{:S(2)}) async-start(), calls=%async_computation.2 | async-start | bytes 2359296 | tf_op jit(solution)/shard_map/all_gather | solution.py:19
  73.0 14.9 %copy-start.1 = (bf16[2,3,16,128]{3,2,1,0:T(8,128)(2,1)S(1)}, bf16[2,3,16,128]{3,2,1,0:T(8,128)(2,1)}, u32[]{:S(2)}) copy-start(bf16[2,3,16,128]{3,2,1,0:T(8,128)(2,1)} %param.7) | copy-start | bytes 73732
  87.9 46.9 %reduce-scatter.4.cloned.1.call-start = ((), (), s32[]{:S(2)}) async-start(), calls=%async_computation.3 | async-start | bytes 196608
  124.1 1.4 copy-start
  124.1 1.4 copy-start.3
Sparse Core Ops, SparseCore 0:
  88.0 27.8 all-gather.1
  127.1 7.6 reduce-scatter.3
where the time goes:
time: 144 us; the launch traced here: 143 us
  local copies, waits for them, and re-layouts  68.5 us (48%)
  waiting for transfers between devices  23.4 us (16%)
  blocking collectives  22.4 us (16%)
  between operations  13.6 us (9%)
  starting transfers between devices  7.63 us (5%)
  other arithmetic  5.83 us (4%)
  matrix products  1.83 us (1%)
    unnamed x13, local copies, waits for them, and re-layouts  30.6 us
    all_gather x1, blocking collectives, local(): weight_rows = lax.all_gather(masked, 'ev', axis=2, tiled=True)  22.4 us
    all_to_all x1, waiting for transfers between devices, local(): lax.all_to_all(selected, 'ev', split_axis=3, concat_axis=2, tiled=True)  15.5 us
    all_to_all x1, local copies, waits for them, and re-layouts, local(): lax.all_to_all(selected, 'ev', split_axis=3, concat_axis=2, tiled=True)  14.8 us
    reshape x1, local copies, waits for them, and re-layouts, local(): selected = selected.reshape(2, 6, event_rows, ev_count * sub_cells)  11.5 us
    unnamed x3, waiting for transfers between devices  7.81 us
    all_to_all x1, starting transfers between devices, local(): lax.all_to_all(selected, 'ev', split_axis=3, concat_axis=2, tiled=True)  7.55 us
    sub x2, local copies, waits for them, and re-layouts, local(): products[0, 0] - products[1, 1]  3.5 us
  transfers between devices with their start and end apart: 3, of which 2 were waited for; matrix products, arithmetic and copies ran while one was open for 10% of the time, Pallas kernels for 0%

commit v1 on v0

--- a/solution.py
+++ b/solution.py
@@ -15,7 +15,10 @@
     shaped = strain.reshape(2, 6, event_rows, ev_count, st_count, sub_cells)
     selected = lax.dynamic_index_in_dim(shaped, lax.axis_index("st"), 4, keepdims=False)
     selected = selected.reshape(2, 6, event_rows, ev_count * sub_cells)
-    narrow = lax.all_to_all(selected, "ev", split_axis=3, concat_axis=2, tiled=True)
+    narrow = jnp.concatenate(
+        lax.all_to_all(jnp.stack(jnp.split(selected, lax.axis_size("ev"), axis=3)), "ev", 0, 0),
+        axis=2,
+    )
     strain_all = lax.all_gather(narrow, "st", axis=3, tiled=True)
     green_flat = green.reshape(2, 3, station_count, 6 * cells_dev)
     voigt = jnp.array([1.0, 1.0, 1.0, 2.0, 2.0, 2.0], jnp.float32)

time: 144 us -> 105 us (0.73)
  local copies, waits for them, and re-layouts: 68.5 us -> 31.9 us
    all_to_all x1 -> x0, local copies, waits for them, and re-layouts: 14.8 us -> none  [local(): lax.all_to_all(selected, 'ev', split_axis=3, concat_axis=2, tiled=True)]
    unnamed x13 -> x28, local copies, waits for them, and re-layouts: 30.6 us -> 16.3 us
    reshape x1, local copies, waits for them, and re-layouts: 11.5 us -> 0.33 us  [local(): selected = selected.reshape(2, 6, event_rows, ev_count * sub_cells)]
    dynamic_slice x1, local copies, waits for them, and re-layouts: 1.89 us -> 4.71 us  [local(): lax.dynamic_index_in_dim(shaped, lax.axis_index('st'), 4, keepdims=False)]
  transfers between devices with their start and end apart: 3 -> 3, of which waited for: 2 -> 2; matrix products, arithmetic and copies ran while one was open for 10% -> 12% of each run, Pallas kernels for 0% -> 0%
where the time goes in v1:
time: 105 us
  local copies, waits for them, and re-layouts  31.9 us (30%)
  waiting for transfers between devices  23.3 us (22%)
  blocking collectives  22.4 us (21%)
  between operations  13.6 us (13%)
  starting transfers between devices  7.5 us (7%)
  other arithmetic  4.4 us (4%)
  matrix products  1.83 us (2%)
    all_gather x1, blocking collectives, local(): weight_rows = lax.all_gather(masked, 'ev', axis=2, tiled=True)  22.4 us
    unnamed x28, local copies, waits for them, and re-layouts  16.3 us
    all_to_all x1, waiting for transfers between devices, local(): lax.all_to_all(jnp.stack(jnp.split(selected, lax.axis_size('ev'), axis=3)...  15.5 us
    unnamed x3, waiting for transfers between devices  7.81 us
    all_to_all x1, starting transfers between devices, local(): lax.all_to_all(jnp.stack(jnp.split(selected, lax.axis_size('ev'), axis=3)...  7.41 us
    dynamic_slice x1, local copies, waits for them, and re-layouts, local(): lax.dynamic_index_in_dim(shaped, lax.axis_index('st'), 4, keepdims=False)  4.71 us
    sub x2, local copies, waits for them, and re-layouts, local(): products[0, 0] - products[1, 1]  3.48 us
    reshape x1, local copies, waits for them, and re-layouts, local(): shaped = strain.reshape(2, 6, event_rows, ev_count, st_count, sub_cells)  2.82 us
  transfers between devices with their start and end apart: 3, of which 2 were waited for; matrix products, arithmetic and copies ran while one was open for 12% of the time, Pallas kernels for 0%

profile of v1, /device:TPU:0, one launch (start us, length us, event | category | flops | bytes accessed | tf_op | source)
XLA Modules:
  0.0 105.0 jit_solution(15221466284462118104)
XLA Ops:
  6.5 2.8 %reshape.26 = bf16[2,6,16,16,2,128]{5,4,3,2,1,0:T(2,128)(2,1)S(1)} reshape(bf16[2,6,16,4096]{3,2,1,0:T(8,128)(2,1)} %param.5) | data formatting | bytes 3145728 | tf_op jit(solution)/shard_map/reshape | solution.py:15
  9.4 4.7 %dynamic-slice_reduce_fusion = bf16[2,6,16,16,128]{4,3,2,1,0:T(8,128)(2,1)S(1)} fusion(bf16[2,6,16,16,2,128]{5,4,3,2,1,0:T(2,128)(2,1)S(1)} %reshape.26, s32[]{:T(128)S(6)} %select_n.4), kind=kLoop, calls=%fused_computation.6 | loop fusion | bytes 1572868 | tf_op jit(solution)/shard_map/jit(dynamic_index_in_dim)/dynamic_slice | solution.py:16
  14.4 0.6 fusion.16
  15.1 0.6 fusion.15
  15.7 0.6 fusion.14
  16.3 0.6 fusion.13
  16.9 0.6 fusion.12
  17.6 0.6 fusion.11
  18.2 0.6 fusion.10
  19.4 0.6 fusion.8
  20.1 0.6 fusion.7
  21.3 0.6 fusion.5
  22.0 0.6 fusion.4
  22.6 0.6 fusion.3
  23.2 0.6 fusion.2
  23.8 0.6 fusion.1
  24.5 7.4 %all-to-all-start = ((bf16[16,2,6,16,128]{4,3,2,1,0:T(8,128)(2,1)}), bf16[16,2,6,16,128]{4,3,2,1,0:T(8,128)(2,1)S(1)}, u32[]{:S(2)}, u32[]{:S(2)}) async-start(bf16[16,2,6,16,128]{4,3,2,1,0:T(8,128)(2,1)} %fusion.1), calls=%async_computation | async-start | bytes 1572864 | tf_op jit(solution)/shard_map/all_to_all | solution.py:19
  31.9 3.1 %copy.44 = bf16[2,3,128,6,256]{2,4,3,1,0:T(8,128)(2,1)S(1)} copy(bf16[2,3,128,6,256]{4,2,3,1,0:T(8,128)(2,1)} %param.6) | data formatting | bytes 4718592 | tf_op args[1]
  35.0 15.5 %all-to-all-done = bf16[16,2,6,16,128]{4,3,2,1,0:T(8,128)(2,1)S(1)} async-done(((bf16[16,2,6,16,128]{4,3,2,1,0:T(8,128)(2,1)}), bf16[16,2,6,16,128]{4,3,2,1,0:T(8,128)(2,1)S(1)}, u32[]{:S(2)}, u32[]{:S(2)}) %all-to-all-start) | async-done | bytes 786464 | tf_op jit(solution)/shard_map/all_to_all | solution.py:19
  50.6 1.1 %copy.43 = bf16[2,6,16,16,128]{4,3,2,1,0:T(8,128)(2,1)} copy(bf16[2,6,16,16,128]{4,3,1,0,2:T(8,128)(2,1)S(1)} %bitcast.108) | data formatting | bytes 1572864 | tf_op jit(solution)/shard_map/reshape | solution.py:18
  51.7 22.4 %all_gather.7 = bf16[2,3,256,128]{3,2,1,0:T(8,128)(2,1)S(1)} all-gather(bf16[2,3,16,128]{3,2,1,0:T(8,128)(2,1)S(1)} %broadcast_multiply_fusion), channel_id=1, replica_groups=mesh['ev'=16,'st'=2] {'ev'}, dimensions={2}, use_global_device_ids=true | all-gather | bytes 417792 | tf_op jit(solution)/shard_map/all_gather | solution.py:25
  74.2 1.8 %convolution_bitcast_fusion = f32[2,2,256,1536]{3,2,1,0:T(8,128)S(1)} fusion(bf16[2,3,128,1536,1]{2,3,1,0,4:T(8,128)(2,1)S(1)} %bitcast.106, bf16[2,3,256,128]{3,2,1,0:T(8,128)(2,1)S(1)} %all_gather.7), kind=kOutput, calls=%fused_computation | convolution fusion | flops 1207959552 | bytes 9043968 | tf_op jit(solution)/shard_map/rfps,qfsn->rqpn/dot_general | solution.py:27
  76.0 1.7 %slice_subtract_fusion = (f32[1,1,256,1536]{3,2,1,0:T(8,128)}, f32[1,1,256,1536]{3,2,1,0:T(8,128)S(1)}) fusion(f32[2,2,256,1536]{3,2,1,0:T(8,128)S(1)} %convolution_bitcast_fusion), kind=kLoop, calls=%fused_computation.3 | loop fusion | flops 786432 | bytes 9437184 | tf_op jit(solution)/shard_map/sub | solution.py:30
  78.2 1.6 %copy.51 = f32[256,6,256]{2,0,1:T(8,128)} copy(f32[256,6,256]{0,2,1:T(8,128)S(1)} %bitcast.102) | data formatting | bytes 3145728 | tf_op jit(solution)/shard_map/add | solution.py:31
  79.8 1.9 %copy.46 = f32[1,1,256,1536]{2,3,1,0:T(8,128)S(1)} copy(f32[1,1,256,1536]{3,2,1,0:T(8,128)} %get-tuple-element.5) | data formatting | bytes 3145728 | tf_op jit(solution)/shard_map/sub | solution.py:30
  81.7 1.6 %copy.50 = f32[256,6,256]{2,0,1:T(8,128)} copy(f32[256,6,256]{0,2,1:T(8,128)S(1)} %bitcast.104) | data formatting | bytes 3145728 | tf_op jit(solution)/shard_map/sub | solution.py:30
  83.7 1.7 %convert_element_type.6 = f32[2,6,256,256]{3,2,1,0:T(8,128)S(1)} convert(bf16[2,6,256,256]{3,2,1,0:T(8,128)(2,1)} %all-gather.2.cloned.1.call-done) | non-fusion elementwise | flops 786432 | bytes 4718592 | tf_op jit(solution)/shard_map/convert_element_type | solution.py:32
  85.8 1.1 %copy-done.1 = f32[256,6,256]{2,0,1:T(8,128)S(1)} copy-done((f32[256,6,256]{2,0,1:T(8,128)S(1)}, f32[256,6,256]{2,0,1:T(8,128)}, u32[]{:S(2)}) %copy-start.1) | copy-done | bytes 1572888
  87.4 0.7 multiply_reduce_fusion
  88.1 0.8 copy.56
  88.9 7.8 %reduce-scatter.4.cloned.1.call-done = f32[128,2]{1,0:T(8,128)} async-done(((f32[256,2]{1,0:T(8,128)}), f32[128,2]{1,0:T(8,128)}) %reduce-scatter.4.cloned.1.call-update) | async-done | bytes 1040
  96.7 1.5 %copy.57 = f32[2,128]{1,0:T(2,128)} copy(f32[2,128]{0,1:T(8,128)} %bitcast.110) | data formatting | bytes 2048
  (28 shorter events, 3.5 us)
Async XLA Ops:
  24.5 26.1 %all-to-all-start = ((bf16[16,2,6,16,128]{4,3,2,1,0:T(8,128)(2,1)}), bf16[16,2,6,16,128]{4,3,2,1,0:T(8,128)(2,1)S(1)}, u32[]{:S(2)}, u32[]{:S(2)}) async-start(bf16[16,2,6,16,128]{4,3,2,1,0:T(8,128)(2,1)} %fusion.1), calls=%async_computation | async-start | bytes 1572864 | tf_op jit(solution)/shard_map/all_to_all | solution.py:19
  31.9 3.1 %copy-start.3 = (s32[16,128]{1,0:T(8,128)S(1)}, s32[16,128]{1,0:T(8,128)}, u32[]{:S(2)}) copy-start(s32[16,128]{1,0:T(8,128)} %param.8) | copy-start | bytes 24580
  31.9 51.8 %all-gather.2.cloned.1.call-start = ((), (), s32[]{:S(2)}) async-start(), calls=%async_computation.2 | async-start | bytes 2359296 | tf_op jit(solution)/shard_map/all_gather | solution.py:22
  35.0 16.7 %copy-start.2 = (bf16[2,3,16,128]{3,2,1,0:T(8,128)(2,1)S(1)}, bf16[2,3,16,128]{3,2,1,0:T(8,128)(2,1)}, u32[]{:S(2)}) copy-start(bf16[2,3,16,128]{3,2,1,0:T(8,128)(2,1)} %param.7) | copy-start | bytes 73732
  51.7 45.1 %reduce-scatter.4.cloned.1.call-start = ((), (), s32[]{:S(2)}) async-start(), calls=%async_computation.3 | async-start | bytes 196608
  85.4 1.4 %copy-start.1 = (f32[256,6,256]{2,0,1:T(8,128)S(1)}, f32[256,6,256]{2,0,1:T(8,128)}, u32[]{:S(2)}) copy-start(f32[256,6,256]{2,0,1:T(8,128)} %copy.50) | copy-start | bytes 4718596
  85.7 1.7 %copy-start = (f32[256,6,256]{2,0,1:T(8,128)S(1)}, f32[256,6,256]{2,0,1:T(8,128)}, u32[]{:S(2)}) copy-start(f32[256,6,256]{2,0,1:T(8,128)} %copy.51) | copy-start | bytes 4718596
  85.7 1.7 %copy-start.4 = (f32[6]{0:T(128)S(1)}, f32[6]{0:T(128)}, u32[]{:S(2)}) copy-start(f32[6]{0:T(128)} %constant.14.clone) | copy-start | bytes 76
Sparse Core Ops, SparseCore 0:
  51.8 27.8 all-gather.1
  89.1 7.6 reduce-scatter.3
